TPU v7x, 32 devices: a whole 2x2x4 slice. The times are simulated.
32 devices in a mesh: cube: 16 (over z, y, x), front: 2 (over core).
Axes of the slice: x: 2, y: 2, z: 4, core: 2. Of those that a mesh axis runs over, the one named last changes fastest.
Arguments:
- elem_loads: float32 [64, 8192], P(None, ('cube', 'front')), may hold values from -6 to 6
- elem_owner: int32 [8192, 1], P(('cube', 'front')), may hold values from 0 to 31; in each aligned block of 256 rows (0 to 255, 256 to 511, ...) at most 16 rows name the same one
- elem_row: int32 [8192], P(('cube', 'front')), may hold values from 0 to 1023
- sep_loads: float32 [4, 64, 512], P(None, None, ('cube', 'front')), may hold values from -6 to 6
- leaf_inverse: float32 [32768, 1024], P(('cube', 'front'))
- leaf_coupling: float32 [64, 32768], P(None, ('cube', 'front')), may hold values from -0.09375 to 0.09375
- coupling0: float32 [512, 512], P(None, ('cube', 'front')), may hold values from -0.25 to 0.25
- coupling1: float32 [256, 512], P(None, ('cube', 'front')), may hold values from -0.375 to 0.375
- coupling2: float32 [128, 512], P(None, ('cube', 'front')), may hold values from -0.5 to 0.5
- inverse0: float32 [512, 512], P(('cube', 'front'))
- inverse1: float32 [512, 256], P(('cube', 'front'))
- inverse2: float32 [512, 128], P(('cube', 'front'))
- inverse3: float32 [512, 64], P(('cube', 'front'))
Outputs:
- leaf_solution: float32 [64, 32768], P(None, ('cube', 'front'))
- sep_solution: float32 [4, 64, 512], P(None, None, ('cube', 'front'))
Inputs may be any that keep to these rules, and one draw needn't show every extreme that they name: `elem_owner`: among the element rows of one device, at most 16 name the same owner, a bound that some block reaches.
All inputs are finite; a program needn't handle non-finite values.
Results may differ from a plain program's by a relative error of at most 0.00012.
Values sent between devices are 32-bit elements; how exact they have to be, the bound alone decides.
A program may use at most 64 MiB of HBM per device.

v0:
```python
import jax
import jax.numpy as jnp
from jax import lax
from jax.sharding import PartitionSpec as P

HIGH = lax.Precision.HIGHEST


def partner(block, axis, apart):
    count = lax.axis_size(axis)
    route = []
    for low in range(count):
        high = low | 1 << apart
        if high != low and high < count:
            route += [(low, high), (high, low)]
    return lax.ppermute(block, axis, route)


def row_dot(left, right):
    return lax.dot_general(left, right, (((1,), (1,)), ((), ())), precision=HIGH)


def mat_dot(left, right):
    return jnp.dot(left, right, precision=HIGH)


def reduce_rows(term, group, position):
    current = term
    for bit in reversed(range(group.bit_length() - 1)):
        half = current.shape[1] // 2
        lower, upper = (current[:, :half], current[:, half:])
        mine = position >> bit & 1 == 1
        keep = jnp.where(mine, upper, lower)
        leave = jnp.where(mine, lower, upper)
        current = keep + partner(leave, ("cube", "front"), bit)
    return current


def gather_rows(local, group, position):
    current = local
    for bit in range(group.bit_length() - 1):
        other = partner(current, ("cube", "front"), bit)
        mine = position >> bit & 1 == 1
        current = jnp.where(
            mine, jnp.concatenate([other, current], 1), jnp.concatenate([current, other], 1)
        )
    return current


def total_rows(term, group):
    current = term
    for bit in range(group.bit_length() - 1):
        current = current + partner(current, ("cube", "front"), bit)
    return current


def shards(
    elem_loads,
    elem_owner,
    elem_row,
    sep_loads,
    leaf_inverse,
    leaf_coupling,
    coupling0,
    coupling1,
    coupling2,
    inverse0,
    inverse1,
    inverse2,
    inverse3,
):
    position = lax.axis_index(("cube", "front"))
    devices = lax.axis_size(("cube", "front"))
    columns = elem_loads.shape[0]
    leaf_rows = leaf_inverse.shape[0]
    sep_rows = sep_loads.shape[2]
    count = elem_owner.shape[0]
    capacity = 2 * count // devices
    owner = elem_owner[:, 0]
    marks = (owner[:, None] == jnp.arange(devices, dtype=jnp.int32)[None, :]).astype(jnp.int32)
    ranks = jnp.sum(jnp.cumsum(marks, axis=0) * marks, axis=1) - 1
    slots = owner * capacity + ranks
    send_vals = jnp.zeros((columns, devices * capacity), jnp.float32).at[:, slots].set(elem_loads)
    send_rows = jnp.full((1, devices * capacity), -1, jnp.int32).at[0, slots].set(elem_row)
    got_vals, got_rows = (
        lax.all_to_all(send_vals, ("cube", "front"), split_axis=1, concat_axis=1, tiled=True),
        lax.all_to_all(send_rows, ("cube", "front"), split_axis=1, concat_axis=1, tiled=True),
    )
    placing = (got_rows[0][:, None] == jnp.arange(leaf_rows, dtype=jnp.int32)[None, :]).astype(
        jnp.float32
    )
    loads = mat_dot(got_vals, placing)
    leaf_y = row_dot(loads, leaf_inverse)
    inverses = [inverse0, inverse1, inverse2, inverse3]
    couplings = [coupling0, coupling1, coupling2, leaf_coupling]
    sep_y = [None] * 4
    child = leaf_y
    for level in (3, 2, 1, 0):
        group = devices >> level
        term = row_dot(child, couplings[level])
        resid = sep_loads[level] - reduce_rows(term, group, position)
        sep_y[level] = row_dot(gather_rows(resid, group, position), inverses[level])
        child = sep_y[level]
    solved = []
    parent = None
    for level in range(4):
        group = devices >> level
        upper = sep_y[level]
        if level > 0:
            upper = upper - mat_dot(parent, couplings[level - 1])
        term = mat_dot(upper, inverses[level])
        parent = total_rows(term, group)
        mine = lax.dynamic_slice_in_dim(parent, position % group * sep_rows, sep_rows, 1)
        solved.append(mine)
    upper = leaf_y - mat_dot(parent, leaf_coupling)
    leaf_solution = mat_dot(upper, leaf_inverse)
    return (leaf_solution, jnp.stack(solved))


def solution(mesh):
    in_specs = (
        P(None, ("cube", "front")),
        P(("cube", "front"), None),
        P(("cube", "front")),
        P(None, None, ("cube", "front")),
        P(("cube", "front"), None),
        P(None, ("cube", "front")),
        P(None, ("cube", "front")),
        P(None, ("cube", "front")),
        P(None, ("cube", "front")),
        P(("cube", "front"), None),
        P(("cube", "front"), None),
        P(("cube", "front"), None),
        P(("cube", "front"), None),
    )
    out_specs = (P(None, ("cube", "front")), P(None, None, ("cube", "front")))
    return jax.shard_map(shards, mesh=mesh, in_specs=in_specs, out_specs=out_specs, check_vma=False)
```

profile of v0, /device:TPU:0, one launch (start us, length us, event | category | flops | bytes accessed | tf_op | source)
XLA Modules:
  0.0 199.2 jit_solution(2309752474257731399)
XLA Ops:
  5.9 7.3 %all-to-all-start.1 = ((s32[1,32,16]{2,0,1:T(1,128)}), s32[1,32,16]{2,0,1:T(1,128)S(1)}, u32[]{:S(2)}, u32[]{:S(2)}) async-start(s32[1,32,16]{2,0,1:T(1,128)} %bitcast.8), calls=%async_computation.1 | async-start | bytes 32768 | tf_op jit(solution)/shard_map/all_to_all | solution.py:87
  16.3 4.1 %all-to-all-done.1 = s32[1,32,16]{2,0,1:T(1,128)S(1)} async-done(((s32[1,32,16]{2,0,1:T(1,128)}), s32[1,32,16]{2,0,1:T(1,128)S(1)}, u32[]{:S(2)}, u32[]{:S(2)}) %all-to-all-start.1) | async-done | bytes 2080 | tf_op jit(solution)/shard_map/all_to_all | solution.py:87
  24.4 6.7 %all-to-all-done = f32[32,1,1024]{2,1,0:T(1,128)S(1)} async-done(((f32[32,1,1024]{2,1,0:T(1,128)}), f32[32,1,1024]{2,1,0:T(1,128)S(1)}, u32[]{:S(2)}, u32[]{:S(2)}) %all-to-all-start) | async-done | bytes 131104 | tf_op jit(solution)/shard_map/all_to_all | solution.py:86
  33.7 6.3 %fusion.41 = f32[64,1024]{1,0:T(8,128)S(1)} fusion(f32[64,1024]{1,0:T(8,128)S(1)} %fusion, f32[1024,1024]{1,0:T(8,128)} %param.17), kind=kOutput, calls=%fused_computation.102 | convolution fusion | flops 805306368 | bytes 4718592 | tf_op jit(solution)/shard_map/dot_general | solution.py:20
  40.8 3.4 %collective-permute-done = f32[64,32]{0,1:T(8,128)S(1)} collective-permute-done((f32[64,32]{0,1:T(8,128)S(1)}, f32[64,32]{0,1:T(8,128)S(1)}, u32[]{:S(2)}, u32[]{:S(2)}) %collective-permute-start) | collective-permute-done | bytes 8224 | tf_op jit(solution)/shard_map/ppermute | solution.py:16
  55.3 3.4 %collective-permute-done.5 = f32[64,32]{0,1:T(8,128)S(1)} collective-permute-done((f32[64,32]{0,1:T(8,128)S(1)}, f32[64,32]{0,1:T(8,128)S(1)}, u32[]{:S(2)}, u32[]{:S(2)}) %collective-permute-start.5) | collective-permute-done | bytes 8224 | tf_op jit(solution)/shard_map/ppermute | solution.py:16
  61.5 3.4 %collective-permute-done.8 = f32[64,32]{0,1:T(8,128)S(1)} collective-permute-done((f32[64,32]{0,1:T(8,128)S(1)}, f32[64,32]{0,1:T(8,128)S(1)}, u32[]{:S(2)}, u32[]{:S(2)}) %collective-permute-start.8) | collective-permute-done | bytes 8224 | tf_op jit(solution)/shard_map/ppermute | solution.py:16
  70.1 3.6 %collective-permute-done.10 = f32[64,128]{0,1:T(8,128)S(1)} collective-permute-done((f32[64,128]{0,1:T(8,128)S(1)}, f32[64,128]{0,1:T(8,128)S(1)}, u32[]{:S(2)}, u32[]{:S(2)}) %collective-permute-start.10) | collective-permute-done | bytes 32800 | tf_op jit(solution)/shard_map/ppermute | solution.py:16
  78.2 3.4 %collective-permute-done.12 = f32[64,32]{0,1:T(8,128)S(1)} collective-permute-done((f32[64,32]{0,1:T(8,128)S(1)}, f32[64,32]{0,1:T(8,128)S(1)}, u32[]{:S(2)}, u32[]{:S(2)}) %collective-permute-start.12) | collective-permute-done | bytes 8224 | tf_op jit(solution)/shard_map/ppermute | solution.py:16
  84.3 3.4 %collective-permute-done.15 = f32[64,32]{0,1:T(8,128)S(1)} collective-permute-done((f32[64,32]{0,1:T(8,128)S(1)}, f32[64,32]{0,1:T(8,128)S(1)}, u32[]{:S(2)}, u32[]{:S(2)}) %collective-permute-start.15) | collective-permute-done | bytes 8224 | tf_op jit(solution)/shard_map/ppermute | solution.py:16
  92.4 3.6 %collective-permute-done.17 = f32[64,128]{0,1:T(8,128)S(1)} collective-permute-done((f32[64,128]{0,1:T(8,128)S(1)}, f32[64,128]{0,1:T(8,128)S(1)}, u32[]{:S(2)}, u32[]{:S(2)}) %collective-permute-start.17) | collective-permute-done | bytes 32800 | tf_op jit(solution)/shard_map/ppermute | solution.py:16
  97.7 6.5 %collective-permute-done.18 = f32[64,256]{0,1:T(8,128)S(1)} collective-permute-done((f32[64,256]{0,1:T(8,128)S(1)}, f32[64,256]{0,1:T(8,128)S(1)}, u32[]{:S(2)}, u32[]{:S(2)}) %collective-permute-start.18) | collective-permute-done | bytes 65568 | tf_op jit(solution)/shard_map/ppermute | solution.py:16
  104.3 4.3 %collective-permute-done.19 = f32[64,128]{0,1:T(8,128)S(1)} collective-permute-done((f32[64,128]{0,1:T(8,128)S(1)}, f32[64,128]{0,1:T(8,128)S(1)}, u32[]{:S(2)}, u32[]{:S(2)}) %collective-permute-start.19) | collective-permute-done | bytes 32800 | tf_op jit(solution)/shard_map/ppermute | solution.py:16
  126.6 4.3 %collective-permute-done.26 = f32[64,128]{0,1:T(8,128)S(1)} collective-permute-done((f32[64,128]{0,1:T(8,128)S(1)}, f32[64,128]{0,1:T(8,128)S(1)}, u32[]{:S(2)}, u32[]{:S(2)}) %collective-permute-start.26) | collective-permute-done | bytes 32800 | tf_op jit(solution)/shard_map/ppermute | solution.py:16
  131.0 7.0 %collective-permute-done.27 = f32[64,256]{0,1:T(8,128)S(1)} collective-permute-done((f32[64,256]{0,1:T(8,128)S(1)}, f32[64,256]{0,1:T(8,128)S(1)}, u32[]{:S(2)}, u32[]{:S(2)}) %collective-permute-start.27) | collective-permute-done | bytes 65568 | tf_op jit(solution)/shard_map/ppermute | solution.py:16
  140.5 5.2 %collective-permute-done.29 = f32[64,512]{1,0:T(8,128)S(1)} collective-permute-done((f32[64,512]{1,0:T(8,128)S(1)}, f32[64,512]{1,0:T(8,128)S(1)}, u32[]{:S(2)}, u32[]{:S(2)}) %collective-permute-start.29) | collective-permute-done | bytes 131104 | tf_op jit(solution)/shard_map/ppermute | solution.py:16
  146.4 4.3 %collective-permute-done.30 = f32[64,512]{1,0:T(8,128)S(1)} collective-permute-done((f32[64,512]{1,0:T(8,128)S(1)}, f32[64,512]{1,0:T(8,128)S(1)}, u32[]{:S(2)}, u32[]{:S(2)}) %collective-permute-start.30) | collective-permute-done | bytes 131104 | tf_op jit(solution)/shard_map/ppermute | solution.py:16
  150.8 5.0 %collective-permute-done.31 = f32[64,512]{1,0:T(8,128)S(1)} collective-permute-done((f32[64,512]{1,0:T(8,128)S(1)}, f32[64,512]{1,0:T(8,128)S(1)}, u32[]{:S(2)}, u32[]{:S(2)}) %collective-permute-start.31) | collective-permute-done | bytes 131104 | tf_op jit(solution)/shard_map/ppermute | solution.py:16
  155.9 6.7 %collective-permute-done.32 = f32[64,512]{1,0:T(8,128)S(1)} collective-permute-done((f32[64,512]{1,0:T(8,128)S(1)}, f32[64,512]{1,0:T(8,128)S(1)}, u32[]{:S(2)}, u32[]{:S(2)}) %collective-permute-start.32) | collective-permute-done | bytes 131104 | tf_op jit(solution)/shard_map/ppermute | solution.py:16
  164.9 3.9 %collective-permute-done.34 = f32[64,256]{1,0:T(8,128)S(1)} collective-permute-done((f32[64,256]{1,0:T(8,128)S(1)}, f32[64,256]{1,0:T(8,128)S(1)}, u32[]{:S(2)}, u32[]{:S(2)}) %collective-permute-start.34) | collective-permute-done | bytes 65568 | tf_op jit(solution)/shard_map/ppermute | solution.py:16
  169.5 3.6 %collective-permute-done.35 = f32[64,256]{1,0:T(8,128)S(1)} collective-permute-done((f32[64,256]{1,0:T(8,128)S(1)}, f32[64,256]{1,0:T(8,128)S(1)}, u32[]{:S(2)}, u32[]{:S(2)}) %collective-permute-start.35) | collective-permute-done | bytes 65568 | tf_op jit(solution)/shard_map/ppermute | solution.py:16
  173.2 4.3 %collective-permute-done.36 = f32[64,256]{1,0:T(8,128)S(1)} collective-permute-done((f32[64,256]{1,0:T(8,128)S(1)}, f32[64,256]{1,0:T(8,128)S(1)}, u32[]{:S(2)}, u32[]{:S(2)}) %collective-permute-start.36) | collective-permute-done | bytes 65568 | tf_op jit(solution)/shard_map/ppermute | solution.py:16
  179.6 3.5 %collective-permute-done.38 = f32[64,128]{1,0:T(8,128)S(1)} collective-permute-done((f32[64,128]{1,0:T(8,128)S(1)}, f32[64,128]{1,0:T(8,128)S(1)}, u32[]{:S(2)}, u32[]{:S(2)}) %collective-permute-start.38) | collective-permute-done | bytes 32800 | tf_op jit(solution)/shard_map/ppermute | solution.py:16
  193.1 5.5 %fusion.50 = f32[64,1024]{1,0:T(8,128)} fusion(f32[64,1024]{1,0:T(8,128)S(1)} %convolution_subtract_fusion, f32[1024,1024]{1,0:T(8,128)} %param.17), kind=kOutput, calls=%fused_computation.111 | convolution fusion | flops 805306368 | bytes 4718592 | tf_op jit(solution)/shard_map/dot_general | solution.py:24
  (180 shorter events, 85.4 us)
Async XLA Ops:
  5.9 14.4 %all-to-all-start.1 = ((s32[1,32,16]{2,0,1:T(1,128)}), s32[1,32,16]{2,0,1:T(1,128)S(1)}, u32[]{:S(2)}, u32[]{:S(2)}) async-start(s32[1,32,16]{2,0,1:T(1,128)} %bitcast.8), calls=%async_computation.1 | async-start | bytes 32768 | tf_op jit(solution)/shard_map/all_to_all | solution.py:87
  20.4 10.8 %all-to-all-start = ((f32[32,1,1024]{2,1,0:T(1,128)}), f32[32,1,1024]{2,1,0:T(1,128)S(1)}, u32[]{:S(2)}, u32[]{:S(2)}) async-start(f32[32,1,1024]{2,1,0:T(1,128)} %reshape.69), calls=%async_computation | async-start | bytes 262144 | tf_op jit(solution)/shard_map/all_to_all | solution.py:86
  50.9 4.0 %collective-permute-start.4 = (f32[64,64]{0,1:T(8,128)S(1)}, f32[64,64]{0,1:T(8,128)S(1)}, u32[]{:S(2)}, u32[]{:S(2)}) collective-permute-start(f32[64,64]{0,1:T(8,128)S(1)} %slice_select_fusion.5), channel_id=1, source_target_pairs={{0,4},{4,0},{1,5},{5,1},{2,6},{6,2},{3,7},{7,3},{8,12},{12,8},{9,1... | collective-permute-start | bytes 49160 | tf_op jit(solution)/shard_map/ppermute | solution.py:16
  64.9 3.9 %collective-permute-start.9 = (f32[64,64]{0,1:T(8,128)S(1)}, f32[64,64]{0,1:T(8,128)S(1)}, u32[]{:S(2)}, u32[]{:S(2)}) collective-permute-start(f32[64,64]{0,1:T(8,128)S(1)} %maximum_select_fusion.11), channel_id=1, source_target_pairs={{0,4},{4,0},{1,5},{5,1},{2,6},{6,2},{3,7},{7,3},{8,12},{12,8},{9,1... | collective-permute-start | bytes 49160 | tf_op jit(solution)/shard_map/ppermute | solution.py:16
  69.4 4.3 %collective-permute-start.10 = (f32[64,128]{0,1:T(8,128)S(1)}, f32[64,128]{0,1:T(8,128)S(1)}, u32[]{:S(2)}, u32[]{:S(2)}) collective-permute-start(f32[64,128]{0,1:T(8,128)S(1)} %slice_select_fusion.2), channel_id=1, source_target_pairs={{0,8},{8,0},{1,9},{9,1},{2,10},{10,2},{3,11},{11,3},{4,12},{12,4},... | collective-permute-start | bytes 98312 | tf_op jit(solution)/shard_map/ppermute | solution.py:16
  73.8 4.0 %collective-permute-start.11 = (f32[64,64]{0,1:T(8,128)S(1)}, f32[64,64]{0,1:T(8,128)S(1)}, u32[]{:S(2)}, u32[]{:S(2)}) collective-permute-start(f32[64,64]{0,1:T(8,128)S(1)} %slice_select_fusion.4), channel_id=1, source_target_pairs={{0,4},{4,0},{1,5},{5,1},{2,6},{6,2},{3,7},{7,3},{8,12},{12,8},{9,1... | collective-permute-start | bytes 49160 | tf_op jit(solution)/shard_map/ppermute | solution.py:16
  87.7 3.9 %collective-permute-start.16 = (f32[64,64]{0,1:T(8,128)S(1)}, f32[64,64]{0,1:T(8,128)S(1)}, u32[]{:S(2)}, u32[]{:S(2)}) collective-permute-start(f32[64,64]{0,1:T(8,128)S(1)} %maximum_select_fusion.12), channel_id=1, source_target_pairs={{0,4},{4,0},{1,5},{5,1},{2,6},{6,2},{3,7},{7,3},{8,12},{12,8},{9,1... | collective-permute-start | bytes 49160 | tf_op jit(solution)/shard_map/ppermute | solution.py:16
  91.7 4.3 %collective-permute-start.17 = (f32[64,128]{0,1:T(8,128)S(1)}, f32[64,128]{0,1:T(8,128)S(1)}, u32[]{:S(2)}, u32[]{:S(2)}) collective-permute-start(f32[64,128]{0,1:T(8,128)S(1)} %maximum_select_fusion.7), channel_id=1, source_target_pairs={{0,8},{8,0},{1,9},{9,1},{2,10},{10,2},{3,11},{11,3},{4,12},{12,4},... | collective-permute-start | bytes 98312 | tf_op jit(solution)/shard_map/ppermute | solution.py:16
  96.8 7.4 %collective-permute-start.18 = (f32[64,256]{0,1:T(8,128)S(1)}, f32[64,256]{0,1:T(8,128)S(1)}, u32[]{:S(2)}, u32[]{:S(2)}) collective-permute-start(f32[64,256]{0,1:T(8,128)S(1)} %slice_select_fusion), channel_id=1, source_target_pairs={{0,16},{16,0},{1,17},{17,1},{2,18},{18,2},{3,19},{19,3},{4,20},{20... | collective-permute-start | bytes 196616 | tf_op jit(solution)/shard_map/ppermute | solution.py:16
  104.3 4.3 %collective-permute-start.19 = (f32[64,128]{0,1:T(8,128)S(1)}, f32[64,128]{0,1:T(8,128)S(1)}, u32[]{:S(2)}, u32[]{:S(2)}) collective-permute-start(f32[64,128]{0,1:T(8,128)S(1)} %slice_select_fusion.1), channel_id=1, source_target_pairs={{0,8},{8,0},{1,9},{9,1},{2,10},{10,2},{3,11},{11,3},{4,12},{12,4},... | collective-permute-start | bytes 98312 | tf_op jit(solution)/shard_map/ppermute | solution.py:16
  108.6 4.0 %collective-permute-start.20 = (f32[64,64]{0,1:T(8,128)S(1)}, f32[64,64]{0,1:T(8,128)S(1)}, u32[]{:S(2)}, u32[]{:S(2)}) collective-permute-start(f32[64,64]{0,1:T(8,128)S(1)} %slice_select_fusion.3), channel_id=1, source_target_pairs={{0,4},{4,0},{1,5},{5,1},{2,6},{6,2},{3,7},{7,3},{8,12},{12,8},{9,1... | collective-permute-start | bytes 49160 | tf_op jit(solution)/shard_map/ppermute | solution.py:16
  122.6 3.9 %collective-permute-start.25 = (f32[64,64]{0,1:T(8,128)S(1)}, f32[64,64]{0,1:T(8,128)S(1)}, u32[]{:S(2)}, u32[]{:S(2)}) collective-permute-start(f32[64,64]{0,1:T(8,128)S(1)} %maximum_select_fusion.13), channel_id=1, source_target_pairs={{0,4},{4,0},{1,5},{5,1},{2,6},{6,2},{3,7},{7,3},{8,12},{12,8},{9,1... | collective-permute-start | bytes 49160 | tf_op jit(solution)/shard_map/ppermute | solution.py:16
  126.5 4.3 %collective-permute-start.26 = (f32[64,128]{0,1:T(8,128)S(1)}, f32[64,128]{0,1:T(8,128)S(1)}, u32[]{:S(2)}, u32[]{:S(2)}) collective-permute-start(f32[64,128]{0,1:T(8,128)S(1)} %maximum_select_fusion.8), channel_id=1, source_target_pairs={{0,8},{8,0},{1,9},{9,1},{2,10},{10,2},{3,11},{11,3},{4,12},{12,4},... | collective-permute-start | bytes 98312 | tf_op jit(solution)/shard_map/ppermute | solution.py:16
  130.9 7.1 %collective-permute-start.27 = (f32[64,256]{0,1:T(8,128)S(1)}, f32[64,256]{0,1:T(8,128)S(1)}, u32[]{:S(2)}, u32[]{:S(2)}) collective-permute-start(f32[64,256]{0,1:T(8,128)S(1)} %maximum_select_fusion.4), channel_id=1, source_target_pairs={{0,16},{16,0},{1,17},{17,1},{2,18},{18,2},{3,19},{19,3},{4,20},{20... | collective-permute-start | bytes 196616 | tf_op jit(solution)/shard_map/ppermute | solution.py:16
  140.0 5.6 %collective-permute-start.29 = (f32[64,512]{1,0:T(8,128)S(1)}, f32[64,512]{1,0:T(8,128)S(1)}, u32[]{:S(2)}, u32[]{:S(2)}) collective-permute-start(f32[64,512]{1,0:T(8,128)S(1)} %add.149), channel_id=1, source_target_pairs={{0,2},{2,0},{1,3},{3,1},{4,6},{6,4},{5,7},{7,5},{8,10},{10,8},{9,1... | collective-permute-start | bytes 393224 | tf_op jit(solution)/shard_map/ppermute | solution.py:16
  145.7 5.0 %collective-permute-start.30 = (f32[64,512]{1,0:T(8,128)S(1)}, f32[64,512]{1,0:T(8,128)S(1)}, u32[]{:S(2)}, u32[]{:S(2)}) collective-permute-start(f32[64,512]{1,0:T(8,128)S(1)} %add.150), channel_id=1, source_target_pairs={{0,4},{4,0},{1,5},{5,1},{2,6},{6,2},{3,7},{7,3},{8,12},{12,8},{9,1... | collective-permute-start | bytes 393224 | tf_op jit(solution)/shard_map/ppermute | solution.py:16
  150.7 5.0 %collective-permute-start.31 = (f32[64,512]{1,0:T(8,128)S(1)}, f32[64,512]{1,0:T(8,128)S(1)}, u32[]{:S(2)}, u32[]{:S(2)}) collective-permute-start(f32[64,512]{1,0:T(8,128)S(1)} %add.151), channel_id=1, source_target_pairs={{0,8},{8,0},{1,9},{9,1},{2,10},{10,2},{3,11},{11,3},{4,12},{12,4},... | collective-permute-start | bytes 393224 | tf_op jit(solution)/shard_map/ppermute | solution.py:16
  155.8 6.8 %collective-permute-start.32 = (f32[64,512]{1,0:T(8,128)S(1)}, f32[64,512]{1,0:T(8,128)S(1)}, u32[]{:S(2)}, u32[]{:S(2)}) collective-permute-start(f32[64,512]{1,0:T(8,128)S(1)} %add.152), channel_id=1, source_target_pairs={{0,16},{16,0},{1,17},{17,1},{2,18},{18,2},{3,19},{19,3},{4,20},{20... | collective-permute-start | bytes 393224 | tf_op jit(solution)/shard_map/ppermute | solution.py:16
  164.4 4.3 %collective-permute-start.34 = (f32[64,256]{1,0:T(8,128)S(1)}, f32[64,256]{1,0:T(8,128)S(1)}, u32[]{:S(2)}, u32[]{:S(2)}) collective-permute-start(f32[64,256]{1,0:T(8,128)S(1)} %add.154), channel_id=1, source_target_pairs={{0,2},{2,0},{1,3},{3,1},{4,6},{6,4},{5,7},{7,5},{8,10},{10,8},{9,1... | collective-permute-start | bytes 196616 | tf_op jit(solution)/shard_map/ppermute | solution.py:16
  168.8 4.3 %collective-permute-start.35 = (f32[64,256]{1,0:T(8,128)S(1)}, f32[64,256]{1,0:T(8,128)S(1)}, u32[]{:S(2)}, u32[]{:S(2)}) collective-permute-start(f32[64,256]{1,0:T(8,128)S(1)} %add.155), channel_id=1, source_target_pairs={{0,4},{4,0},{1,5},{5,1},{2,6},{6,2},{3,7},{7,3},{8,12},{12,8},{9,1... | collective-permute-start | bytes 196616 | tf_op jit(solution)/shard_map/ppermute | solution.py:16
  173.1 4.3 %collective-permute-start.36 = (f32[64,256]{1,0:T(8,128)S(1)}, f32[64,256]{1,0:T(8,128)S(1)}, u32[]{:S(2)}, u32[]{:S(2)}) collective-permute-start(f32[64,256]{1,0:T(8,128)S(1)} %add.156), channel_id=1, source_target_pairs={{0,8},{8,0},{1,9},{9,1},{2,10},{10,2},{3,11},{11,3},{4,12},{12,4},... | collective-permute-start | bytes 196616 | tf_op jit(solution)/shard_map/ppermute | solution.py:16
  179.2 3.9 %collective-permute-start.38 = (f32[64,128]{1,0:T(8,128)S(1)}, f32[64,128]{1,0:T(8,128)S(1)}, u32[]{:S(2)}, u32[]{:S(2)}) collective-permute-start(f32[64,128]{1,0:T(8,128)S(1)} %add.158), channel_id=1, source_target_pairs={{0,2},{2,0},{1,3},{3,1},{4,6},{6,4},{5,7},{7,5},{8,10},{10,8},{9,1... | collective-permute-start | bytes 98312 | tf_op jit(solution)/shard_map/ppermute | solution.py:16
  183.1 3.9 %collective-permute-start.39 = (f32[64,128]{1,0:T(8,128)S(1)}, f32[64,128]{1,0:T(8,128)S(1)}, u32[]{:S(2)}, u32[]{:S(2)}) collective-permute-start(f32[64,128]{1,0:T(8,128)S(1)} %add.159), channel_id=1, source_target_pairs={{0,4},{4,0},{1,5},{5,1},{2,6},{6,2},{3,7},{7,3},{8,12},{12,8},{9,1... | collective-permute-start | bytes 98312 | tf_op jit(solution)/shard_map/ppermute | solution.py:16
  188.7 3.9 %collective-permute-start.41 = (f32[64,64]{0,1:T(8,128)S(1)}, f32[64,64]{0,1:T(8,128)S(1)}, u32[]{:S(2)}, u32[]{:S(2)}) collective-permute-start(f32[64,64]{0,1:T(8,128)S(1)} %add.161), channel_id=1, source_target_pairs={{0,2},{2,0},{1,3},{3,1},{4,6},{6,4},{5,7},{7,5},{8,10},{10,8},{9,1... | collective-permute-start | bytes 49160 | tf_op jit(solution)/shard_map/ppermute | solution.py:16
  (29 other events, 568.2 us)
where the time goes:
time: 200 us; the launch traced here: 199 us
  waiting for transfers between devices  143 us (72%)
  starting transfers between devices  25 us (12%)
  matrix products  17.2 us (9%)
  local copies, waits for them, and re-layouts  7.1 us (4%)
  other arithmetic  5.52 us (3%)
    ppermute x42, waiting for transfers between devices, partner(): return lax.ppermute(block, axis, route)  132 us
    ppermute x42, starting transfers between devices, partner(): return lax.ppermute(block, axis, route)  14.9 us
    dot_general x9, matrix products, row_dot(): lax.dot_general(left, right, (((1,), (1,)), ((), ())), precision=HIGH)  8.69 us
    dot_general x10, matrix products, mat_dot(): return jnp.dot(left, right, precision=HIGH)  8.56 us
    all_to_all x1, starting transfers between devices, shards(): lax.all_to_all(send_rows, ('cube', 'front'), split_axis=1, concat_axis=1,...  7.33 us
    all_to_all x1, waiting for transfers between devices, shards(): lax.all_to_all(send_vals, ('cube', 'front'), split_axis=1, concat_axis=1,...  6.73 us
    all_to_all x1, waiting for transfers between devices, shards(): lax.all_to_all(send_rows, ('cube', 'front'), split_axis=1, concat_axis=1,...  4.08 us
  transfers between devices with their start and end apart: 44, of which 44 were waited for; matrix products, arithmetic and copies ran while one was open for 2% of the time, Pallas kernels for 0%

commit v1 on v0

--- a/solution.py
+++ b/solution.py
@@ -84,7 +84,15 @@
     send_rows = jnp.full((1, devices * capacity), -1, jnp.int32).at[0, slots].set(elem_row)
     got_vals, got_rows = (
         lax.all_to_all(send_vals, ("cube", "front"), split_axis=1, concat_axis=1, tiled=True),
-        lax.all_to_all(send_rows, ("cube", "front"), split_axis=1, concat_axis=1, tiled=True),
+        jnp.concatenate(
+            lax.all_to_all(
+                jnp.stack(jnp.split(send_rows, lax.axis_size(("cube", "front")), axis=1)),
+                ("cube", "front"),
+                0,
+                0,
+            ),
+            axis=1,
+        ),
     )
     placing = (got_rows[0][:, None] == jnp.arange(leaf_rows, dtype=jnp.int32)[None, :]).astype(
         jnp.float32

time: 200 us -> 217 us (1.085)
  local copies, waits for them, and re-layouts: 7.1 us -> 24.7 us
    unnamed x21 -> x52, local copies, waits for them, and re-layouts: 1.92 us -> 19.6 us
where the time goes in v1:
time: 217 us
  waiting for transfers between devices  143 us (66%)
  starting transfers between devices  25.1 us (12%)
  local copies, waits for them, and re-layouts  24.7 us (11%)
  matrix products  17.5 us (8%)
  other arithmetic  5.52 us (3%)
    ppermute x42, waiting for transfers between devices, partner(): return lax.ppermute(block, axis, route)  132 us
    unnamed x52, local copies, waits for them, and re-layouts  19.6 us
    ppermute x42, starting transfers between devices, partner(): return lax.ppermute(block, axis, route)  15 us
    dot_general x9, matrix products, row_dot(): lax.dot_general(left, right, (((1,), (1,)), ((), ())), precision=HIGH)  9 us
    dot_general x10, matrix products, mat_dot(): return jnp.dot(left, right, precision=HIGH)  8.47 us
    all_to_all x1, starting transfers between devices, shards(): lax.all_to_all(jnp.stack(jnp.split(send_rows, lax.axis_size(('cube', 'fro...  7.33 us
    all_to_all x1, waiting for transfers between devices, shards(): lax.all_to_all(send_vals, ('cube', 'front'), split_axis=1, concat_axis=1,...  6.73 us
  transfers between devices with their start and end apart: 44, of which 44 were waited for; matrix products, arithmetic and copies ran while one was open for 2% of the time, Pallas kernels for 0%

profile of v1, /device:TPU:0, one launch (start us, length us, event | category | flops | bytes accessed | tf_op | source)
XLA Modules:
  0.0 217.1 jit_solution(8135433554811807445)
XLA Ops:
  23.5 7.3 %all-to-all-start.1 = ((s32[32,1,16]{2,1,0:T(1,128)}), s32[32,1,16]{2,1,0:T(1,128)S(1)}, u32[]{:S(2)}, u32[]{:S(2)}) async-start(s32[32,1,16]{2,1,0:T(1,128)} %constant_dynamic-update-slice_fusion), calls=%async_computation.1 | async-start | bytes 32768 | tf_op jit(solution)/shard_map/all_to_all | solution.py:88
  33.9 4.1 %all-to-all-done.1 = s32[32,1,16]{2,1,0:T(1,128)S(1)} async-done(((s32[32,1,16]{2,1,0:T(1,128)}), s32[32,1,16]{2,1,0:T(1,128)S(1)}, u32[]{:S(2)}, u32[]{:S(2)}) %all-to-all-start.1) | async-done | bytes 2080 | tf_op jit(solution)/shard_map/all_to_all | solution.py:88
  42.0 6.7 %all-to-all-done = f32[32,1,1024]{2,1,0:T(1,128)S(1)} async-done(((f32[32,1,1024]{2,1,0:T(1,128)}), f32[32,1,1024]{2,1,0:T(1,128)S(1)}, u32[]{:S(2)}, u32[]{:S(2)}) %all-to-all-start) | async-done | bytes 131104 | tf_op jit(solution)/shard_map/all_to_all | solution.py:86
  51.4 6.3 %fusion.41 = f32[64,1024]{1,0:T(8,128)S(1)} fusion(f32[64,1024]{1,0:T(8,128)S(1)} %fusion, f32[1024,1024]{1,0:T(8,128)} %param.17), kind=kOutput, calls=%fused_computation.166 | convolution fusion | flops 805306368 | bytes 4718592 | tf_op jit(solution)/shard_map/dot_general | solution.py:20
  58.4 3.4 %collective-permute-done = f32[64,32]{0,1:T(8,128)S(1)} collective-permute-done((f32[64,32]{0,1:T(8,128)S(1)}, f32[64,32]{0,1:T(8,128)S(1)}, u32[]{:S(2)}, u32[]{:S(2)}) %collective-permute-start) | collective-permute-done | bytes 8224 | tf_op jit(solution)/shard_map/ppermute | solution.py:16
  64.7 3.4 %collective-permute-done.3 = f32[64,32]{0,1:T(8,128)S(1)} collective-permute-done((f32[64,32]{0,1:T(8,128)S(1)}, f32[64,32]{0,1:T(8,128)S(1)}, u32[]{:S(2)}, u32[]{:S(2)}) %collective-permute-start.3) | collective-permute-done | bytes 8224 | tf_op jit(solution)/shard_map/ppermute | solution.py:16
  72.9 3.4 %collective-permute-done.5 = f32[64,32]{0,1:T(8,128)S(1)} collective-permute-done((f32[64,32]{0,1:T(8,128)S(1)}, f32[64,32]{0,1:T(8,128)S(1)}, u32[]{:S(2)}, u32[]{:S(2)}) %collective-permute-start.5) | collective-permute-done | bytes 8224 | tf_op jit(solution)/shard_map/ppermute | solution.py:16
  79.1 3.4 %collective-permute-done.8 = f32[64,32]{0,1:T(8,128)S(1)} collective-permute-done((f32[64,32]{0,1:T(8,128)S(1)}, f32[64,32]{0,1:T(8,128)S(1)}, u32[]{:S(2)}, u32[]{:S(2)}) %collective-permute-start.8) | collective-permute-done | bytes 8224 | tf_op jit(solution)/shard_map/ppermute | solution.py:16
  87.7 3.6 %collective-permute-done.10 = f32[64,128]{0,1:T(8,128)S(1)} collective-permute-done((f32[64,128]{0,1:T(8,128)S(1)}, f32[64,128]{0,1:T(8,128)S(1)}, u32[]{:S(2)}, u32[]{:S(2)}) %collective-permute-start.10) | collective-permute-done | bytes 32800 | tf_op jit(solution)/shard_map/ppermute | solution.py:16
  110.0 3.6 %collective-permute-done.17 = f32[64,128]{0,1:T(8,128)S(1)} collective-permute-done((f32[64,128]{0,1:T(8,128)S(1)}, f32[64,128]{0,1:T(8,128)S(1)}, u32[]{:S(2)}, u32[]{:S(2)}) %collective-permute-start.17) | collective-permute-done | bytes 32800 | tf_op jit(solution)/shard_map/ppermute | solution.py:16
  115.3 6.5 %collective-permute-done.18 = f32[64,256]{0,1:T(8,128)S(1)} collective-permute-done((f32[64,256]{0,1:T(8,128)S(1)}, f32[64,256]{0,1:T(8,128)S(1)}, u32[]{:S(2)}, u32[]{:S(2)}) %collective-permute-start.18) | collective-permute-done | bytes 65568 | tf_op jit(solution)/shard_map/ppermute | solution.py:16
  122.0 4.3 %collective-permute-done.19 = f32[64,128]{0,1:T(8,128)S(1)} collective-permute-done((f32[64,128]{0,1:T(8,128)S(1)}, f32[64,128]{0,1:T(8,128)S(1)}, u32[]{:S(2)}, u32[]{:S(2)}) %collective-permute-start.19) | collective-permute-done | bytes 32800 | tf_op jit(solution)/shard_map/ppermute | solution.py:16
  144.2 4.3 %collective-permute-done.26 = f32[64,128]{0,1:T(8,128)S(1)} collective-permute-done((f32[64,128]{0,1:T(8,128)S(1)}, f32[64,128]{0,1:T(8,128)S(1)}, u32[]{:S(2)}, u32[]{:S(2)}) %collective-permute-start.26) | collective-permute-done | bytes 32800 | tf_op jit(solution)/shard_map/ppermute | solution.py:16
  148.6 7.0 %collective-permute-done.27 = f32[64,256]{0,1:T(8,128)S(1)} collective-permute-done((f32[64,256]{0,1:T(8,128)S(1)}, f32[64,256]{0,1:T(8,128)S(1)}, u32[]{:S(2)}, u32[]{:S(2)}) %collective-permute-start.27) | collective-permute-done | bytes 65568 | tf_op jit(solution)/shard_map/ppermute | solution.py:16
  158.3 5.2 %collective-permute-done.29 = f32[64,512]{1,0:T(8,128)S(1)} collective-permute-done((f32[64,512]{1,0:T(8,128)S(1)}, f32[64,512]{1,0:T(8,128)S(1)}, u32[]{:S(2)}, u32[]{:S(2)}) %collective-permute-start.29) | collective-permute-done | bytes 131104 | tf_op jit(solution)/shard_map/ppermute | solution.py:16
  164.2 4.3 %collective-permute-done.30 = f32[64,512]{1,0:T(8,128)S(1)} collective-permute-done((f32[64,512]{1,0:T(8,128)S(1)}, f32[64,512]{1,0:T(8,128)S(1)}, u32[]{:S(2)}, u32[]{:S(2)}) %collective-permute-start.30) | collective-permute-done | bytes 131104 | tf_op jit(solution)/shard_map/ppermute | solution.py:16
  168.7 5.0 %collective-permute-done.31 = f32[64,512]{1,0:T(8,128)S(1)} collective-permute-done((f32[64,512]{1,0:T(8,128)S(1)}, f32[64,512]{1,0:T(8,128)S(1)}, u32[]{:S(2)}, u32[]{:S(2)}) %collective-permute-start.31) | collective-permute-done | bytes 131104 | tf_op jit(solution)/shard_map/ppermute | solution.py:16
  173.7 6.7 %collective-permute-done.32 = f32[64,512]{1,0:T(8,128)S(1)} collective-permute-done((f32[64,512]{1,0:T(8,128)S(1)}, f32[64,512]{1,0:T(8,128)S(1)}, u32[]{:S(2)}, u32[]{:S(2)}) %collective-permute-start.32) | collective-permute-done | bytes 131104 | tf_op jit(solution)/shard_map/ppermute | solution.py:16
  182.8 3.9 %collective-permute-done.34 = f32[64,256]{1,0:T(8,128)S(1)} collective-permute-done((f32[64,256]{1,0:T(8,128)S(1)}, f32[64,256]{1,0:T(8,128)S(1)}, u32[]{:S(2)}, u32[]{:S(2)}) %collective-permute-start.34) | collective-permute-done | bytes 65568 | tf_op jit(solution)/shard_map/ppermute | solution.py:16
  187.4 3.6 %collective-permute-done.35 = f32[64,256]{1,0:T(8,128)S(1)} collective-permute-done((f32[64,256]{1,0:T(8,128)S(1)}, f32[64,256]{1,0:T(8,128)S(1)}, u32[]{:S(2)}, u32[]{:S(2)}) %collective-permute-start.35) | collective-permute-done | bytes 65568 | tf_op jit(solution)/shard_map/ppermute | solution.py:16
  191.1 4.3 %collective-permute-done.36 = f32[64,256]{1,0:T(8,128)S(1)} collective-permute-done((f32[64,256]{1,0:T(8,128)S(1)}, f32[64,256]{1,0:T(8,128)S(1)}, u32[]{:S(2)}, u32[]{:S(2)}) %collective-permute-start.36) | collective-permute-done | bytes 65568 | tf_op jit(solution)/shard_map/ppermute | solution.py:16
  197.4 3.5 %collective-permute-done.38 = f32[64,128]{1,0:T(8,128)S(1)} collective-permute-done((f32[64,128]{1,0:T(8,128)S(1)}, f32[64,128]{1,0:T(8,128)S(1)}, u32[]{:S(2)}, u32[]{:S(2)}) %collective-permute-start.38) | collective-permute-done | bytes 32800 | tf_op jit(solution)/shard_map/ppermute | solution.py:16
  207.1 3.4 %collective-permute-done.41 = f32[64,64]{0,1:T(8,128)S(1)} collective-permute-done((f32[64,64]{0,1:T(8,128)S(1)}, f32[64,64]{0,1:T(8,128)S(1)}, u32[]{:S(2)}, u32[]{:S(2)}) %collective-permute-start.41) | collective-permute-done | bytes 16416 | tf_op jit(solution)/shard_map/ppermute | solution.py:16
  210.9 5.5 %fusion.50 = f32[64,1024]{1,0:T(8,128)} fusion(f32[64,1024]{1,0:T(8,128)S(1)} %convolution_subtract_fusion, f32[1024,1024]{1,0:T(8,128)} %param.17), kind=kOutput, calls=%fused_computation.175 | convolution fusion | flops 805306368 | bytes 4718592 | tf_op jit(solution)/shard_map/dot_general | solution.py:24
  (211 shorter events, 103.3 us)
Async XLA Ops:
  23.5 14.4 %all-to-all-start.1 = ((s32[32,1,16]{2,1,0:T(1,128)}), s32[32,1,16]{2,1,0:T(1,128)S(1)}, u32[]{:S(2)}, u32[]{:S(2)}) async-start(s32[32,1,16]{2,1,0:T(1,128)} %constant_dynamic-update-slice_fusion), calls=%async_computation.1 | async-start | bytes 32768 | tf_op jit(solution)/shard_map/all_to_all | solution.py:88
  38.0 10.8 %all-to-all-start = ((f32[32,1,1024]{2,1,0:T(1,128)}), f32[32,1,1024]{2,1,0:T(1,128)S(1)}, u32[]{:S(2)}, u32[]{:S(2)}) async-start(f32[32,1,1024]{2,1,0:T(1,128)} %reshape.65), calls=%async_computation | async-start | bytes 262144 | tf_op jit(solution)/shard_map/all_to_all | solution.py:86
  68.5 4.0 %collective-permute-start.4 = (f32[64,64]{0,1:T(8,128)S(1)}, f32[64,64]{0,1:T(8,128)S(1)}, u32[]{:S(2)}, u32[]{:S(2)}) collective-permute-start(f32[64,64]{0,1:T(8,128)S(1)} %slice_select_fusion.5), channel_id=1, source_target_pairs={{0,4},{4,0},{1,5},{5,1},{2,6},{6,2},{3,7},{7,3},{8,12},{12,8},{9,1... | collective-permute-start | bytes 49160 | tf_op jit(solution)/shard_map/ppermute | solution.py:16
  82.5 3.9 %collective-permute-start.9 = (f32[64,64]{0,1:T(8,128)S(1)}, f32[64,64]{0,1:T(8,128)S(1)}, u32[]{:S(2)}, u32[]{:S(2)}) collective-permute-start(f32[64,64]{0,1:T(8,128)S(1)} %maximum_select_fusion.11), channel_id=1, source_target_pairs={{0,4},{4,0},{1,5},{5,1},{2,6},{6,2},{3,7},{7,3},{8,12},{12,8},{9,1... | collective-permute-start | bytes 49160 | tf_op jit(solution)/shard_map/ppermute | solution.py:16
  87.0 4.3 %collective-permute-start.10 = (f32[64,128]{0,1:T(8,128)S(1)}, f32[64,128]{0,1:T(8,128)S(1)}, u32[]{:S(2)}, u32[]{:S(2)}) collective-permute-start(f32[64,128]{0,1:T(8,128)S(1)} %slice_select_fusion.2), channel_id=1, source_target_pairs={{0,8},{8,0},{1,9},{9,1},{2,10},{10,2},{3,11},{11,3},{4,12},{12,4},... | collective-permute-start | bytes 98312 | tf_op jit(solution)/shard_map/ppermute | solution.py:16
  91.4 4.0 %collective-permute-start.11 = (f32[64,64]{0,1:T(8,128)S(1)}, f32[64,64]{0,1:T(8,128)S(1)}, u32[]{:S(2)}, u32[]{:S(2)}) collective-permute-start(f32[64,64]{0,1:T(8,128)S(1)} %slice_select_fusion.4), channel_id=1, source_target_pairs={{0,4},{4,0},{1,5},{5,1},{2,6},{6,2},{3,7},{7,3},{8,12},{12,8},{9,1... | collective-permute-start | bytes 49160 | tf_op jit(solution)/shard_map/ppermute | solution.py:16
  105.4 3.9 %collective-permute-start.16 = (f32[64,64]{0,1:T(8,128)S(1)}, f32[64,64]{0,1:T(8,128)S(1)}, u32[]{:S(2)}, u32[]{:S(2)}) collective-permute-start(f32[64,64]{0,1:T(8,128)S(1)} %maximum_select_fusion.12), channel_id=1, source_target_pairs={{0,4},{4,0},{1,5},{5,1},{2,6},{6,2},{3,7},{7,3},{8,12},{12,8},{9,1... | collective-permute-start | bytes 49160 | tf_op jit(solution)/shard_map/ppermute | solution.py:16
  109.3 4.3 %collective-permute-start.17 = (f32[64,128]{0,1:T(8,128)S(1)}, f32[64,128]{0,1:T(8,128)S(1)}, u32[]{:S(2)}, u32[]{:S(2)}) collective-permute-start(f32[64,128]{0,1:T(8,128)S(1)} %maximum_select_fusion.7), channel_id=1, source_target_pairs={{0,8},{8,0},{1,9},{9,1},{2,10},{10,2},{3,11},{11,3},{4,12},{12,4},... | collective-permute-start | bytes 98312 | tf_op jit(solution)/shard_map/ppermute | solution.py:16
  114.5 7.4 %collective-permute-start.18 = (f32[64,256]{0,1:T(8,128)S(1)}, f32[64,256]{0,1:T(8,128)S(1)}, u32[]{:S(2)}, u32[]{:S(2)}) collective-permute-start(f32[64,256]{0,1:T(8,128)S(1)} %slice_select_fusion), channel_id=1, source_target_pairs={{0,16},{16,0},{1,17},{17,1},{2,18},{18,2},{3,19},{19,3},{4,20},{20... | collective-permute-start | bytes 196616 | tf_op jit(solution)/shard_map/ppermute | solution.py:16
  121.9 4.3 %collective-permute-start.19 = (f32[64,128]{0,1:T(8,128)S(1)}, f32[64,128]{0,1:T(8,128)S(1)}, u32[]{:S(2)}, u32[]{:S(2)}) collective-permute-start(f32[64,128]{0,1:T(8,128)S(1)} %slice_select_fusion.1), channel_id=1, source_target_pairs={{0,8},{8,0},{1,9},{9,1},{2,10},{10,2},{3,11},{11,3},{4,12},{12,4},... | collective-permute-start | bytes 98312 | tf_op jit(solution)/shard_map/ppermute | solution.py:16
  126.2 4.0 %collective-permute-start.20 = (f32[64,64]{0,1:T(8,128)S(1)}, f32[64,64]{0,1:T(8,128)S(1)}, u32[]{:S(2)}, u32[]{:S(2)}) collective-permute-start(f32[64,64]{0,1:T(8,128)S(1)} %slice_select_fusion.3), channel_id=1, source_target_pairs={{0,4},{4,0},{1,5},{5,1},{2,6},{6,2},{3,7},{7,3},{8,12},{12,8},{9,1... | collective-permute-start | bytes 49160 | tf_op jit(solution)/shard_map/ppermute | solution.py:16
  140.2 3.9 %collective-permute-start.25 = (f32[64,64]{0,1:T(8,128)S(1)}, f32[64,64]{0,1:T(8,128)S(1)}, u32[]{:S(2)}, u32[]{:S(2)}) collective-permute-start(f32[64,64]{0,1:T(8,128)S(1)} %maximum_select_fusion.13), channel_id=1, source_target_pairs={{0,4},{4,0},{1,5},{5,1},{2,6},{6,2},{3,7},{7,3},{8,12},{12,8},{9,1... | collective-permute-start | bytes 49160 | tf_op jit(solution)/shard_map/ppermute | solution.py:16
  144.2 4.3 %collective-permute-start.26 = (f32[64,128]{0,1:T(8,128)S(1)}, f32[64,128]{0,1:T(8,128)S(1)}, u32[]{:S(2)}, u32[]{:S(2)}) collective-permute-start(f32[64,128]{0,1:T(8,128)S(1)} %maximum_select_fusion.8), channel_id=1, source_target_pairs={{0,8},{8,0},{1,9},{9,1},{2,10},{10,2},{3,11},{11,3},{4,12},{12,4},... | collective-permute-start | bytes 98312 | tf_op jit(solution)/shard_map/ppermute | solution.py:16
  148.5 7.1 %collective-permute-start.27 = (f32[64,256]{0,1:T(8,128)S(1)}, f32[64,256]{0,1:T(8,128)S(1)}, u32[]{:S(2)}, u32[]{:S(2)}) collective-permute-start(f32[64,256]{0,1:T(8,128)S(1)} %maximum_select_fusion.4), channel_id=1, source_target_pairs={{0,16},{16,0},{1,17},{17,1},{2,18},{18,2},{3,19},{19,3},{4,20},{20... | collective-permute-start | bytes 196616 | tf_op jit(solution)/shard_map/ppermute | solution.py:16
  157.9 5.6 %collective-permute-start.29 = (f32[64,512]{1,0:T(8,128)S(1)}, f32[64,512]{1,0:T(8,128)S(1)}, u32[]{:S(2)}, u32[]{:S(2)}) collective-permute-start(f32[64,512]{1,0:T(8,128)S(1)} %add.149), channel_id=1, source_target_pairs={{0,2},{2,0},{1,3},{3,1},{4,6},{6,4},{5,7},{7,5},{8,10},{10,8},{9,1... | collective-permute-start | bytes 393224 | tf_op jit(solution)/shard_map/ppermute | solution.py:16
  163.5 5.0 %collective-permute-start.30 = (f32[64,512]{1,0:T(8,128)S(1)}, f32[64,512]{1,0:T(8,128)S(1)}, u32[]{:S(2)}, u32[]{:S(2)}) collective-permute-start(f32[64,512]{1,0:T(8,128)S(1)} %add.150), channel_id=1, source_target_pairs={{0,4},{4,0},{1,5},{5,1},{2,6},{6,2},{3,7},{7,3},{8,12},{12,8},{9,1... | collective-permute-start | bytes 393224 | tf_op jit(solution)/shard_map/ppermute | solution.py:16
  168.6 5.0 %collective-permute-start.31 = (f32[64,512]{1,0:T(8,128)S(1)}, f32[64,512]{1,0:T(8,128)S(1)}, u32[]{:S(2)}, u32[]{:S(2)}) collective-permute-start(f32[64,512]{1,0:T(8,128)S(1)} %add.151), channel_id=1, source_target_pairs={{0,8},{8,0},{1,9},{9,1},{2,10},{10,2},{3,11},{11,3},{4,12},{12,4},... | collective-permute-start | bytes 393224 | tf_op jit(solution)/shard_map/ppermute | solution.py:16
  173.6 6.8 %collective-permute-start.32 = (f32[64,512]{1,0:T(8,128)S(1)}, f32[64,512]{1,0:T(8,128)S(1)}, u32[]{:S(2)}, u32[]{:S(2)}) collective-permute-start(f32[64,512]{1,0:T(8,128)S(1)} %add.152), channel_id=1, source_target_pairs={{0,16},{16,0},{1,17},{17,1},{2,18},{18,2},{3,19},{19,3},{4,20},{20... | collective-permute-start | bytes 393224 | tf_op jit(solution)/shard_map/ppermute | solution.py:16
  182.3 4.3 %collective-permute-start.34 = (f32[64,256]{1,0:T(8,128)S(1)}, f32[64,256]{1,0:T(8,128)S(1)}, u32[]{:S(2)}, u32[]{:S(2)}) collective-permute-start(f32[64,256]{1,0:T(8,128)S(1)} %add.154), channel_id=1, source_target_pairs={{0,2},{2,0},{1,3},{3,1},{4,6},{6,4},{5,7},{7,5},{8,10},{10,8},{9,1... | collective-permute-start | bytes 196616 | tf_op jit(solution)/shard_map/ppermute | solution.py:16
  186.6 4.3 %collective-permute-start.35 = (f32[64,256]{1,0:T(8,128)S(1)}, f32[64,256]{1,0:T(8,128)S(1)}, u32[]{:S(2)}, u32[]{:S(2)}) collective-permute-start(f32[64,256]{1,0:T(8,128)S(1)} %add.155), channel_id=1, source_target_pairs={{0,4},{4,0},{1,5},{5,1},{2,6},{6,2},{3,7},{7,3},{8,12},{12,8},{9,1... | collective-permute-start | bytes 196616 | tf_op jit(solution)/shard_map/ppermute | solution.py:16
  191.0 4.3 %collective-permute-start.36 = (f32[64,256]{1,0:T(8,128)S(1)}, f32[64,256]{1,0:T(8,128)S(1)}, u32[]{:S(2)}, u32[]{:S(2)}) collective-permute-start(f32[64,256]{1,0:T(8,128)S(1)} %add.156), channel_id=1, source_target_pairs={{0,8},{8,0},{1,9},{9,1},{2,10},{10,2},{3,11},{11,3},{4,12},{12,4},... | collective-permute-start | bytes 196616 | tf_op jit(solution)/shard_map/ppermute | solution.py:16
  197.0 3.9 %collective-permute-start.38 = (f32[64,128]{1,0:T(8,128)S(1)}, f32[64,128]{1,0:T(8,128)S(1)}, u32[]{:S(2)}, u32[]{:S(2)}) collective-permute-start(f32[64,128]{1,0:T(8,128)S(1)} %add.158), channel_id=1, source_target_pairs={{0,2},{2,0},{1,3},{3,1},{4,6},{6,4},{5,7},{7,5},{8,10},{10,8},{9,1... | collective-permute-start | bytes 98312 | tf_op jit(solution)/shard_map/ppermute | solution.py:16
  201.0 3.9 %collective-permute-start.39 = (f32[64,128]{1,0:T(8,128)S(1)}, f32[64,128]{1,0:T(8,128)S(1)}, u32[]{:S(2)}, u32[]{:S(2)}) collective-permute-start(f32[64,128]{1,0:T(8,128)S(1)} %add.159), channel_id=1, source_target_pairs={{0,4},{4,0},{1,5},{5,1},{2,6},{6,2},{3,7},{7,3},{8,12},{12,8},{9,1... | collective-permute-start | bytes 98312 | tf_op jit(solution)/shard_map/ppermute | solution.py:16
  206.6 3.9 %collective-permute-start.41 = (f32[64,64]{0,1:T(8,128)S(1)}, f32[64,64]{0,1:T(8,128)S(1)}, u32[]{:S(2)}, u32[]{:S(2)}) collective-permute-start(f32[64,64]{0,1:T(8,128)S(1)} %add.161), channel_id=1, source_target_pairs={{0,2},{2,0},{1,3},{3,1},{4,6},{6,4},{5,7},{7,5},{8,10},{10,8},{9,1... | collective-permute-start | bytes 49160 | tf_op jit(solution)/shard_map/ppermute | solution.py:16
  (29 other events, 638.7 us)
